TPU v7x, 32 devices: a whole 2x2x4 slice. The times are simulated.
32 devices in a mesh: seq: 4 (over z), dp: 8 (over y, x, core).
Axes of the slice: x: 2, y: 2, z: 4, core: 2. Of those that a mesh axis runs over, the one named last changes fastest.
Arguments:
- hidden_in: bfloat16 [16, 2048, 1024], P('dp', 'seq'), may hold values from -6 to 6
- mixer_weights: float32 [1, 5, 1024, 1024], P(None, None, 'dp'), may hold values from -0.1875 to 0.1875
- channel_in_weights: float32 [1, 2, 1024, 2816], P(None, None, 'dp'), may hold values from -0.1875 to 0.1875
- channel_out_weights: float32 [1, 2816, 1024], P(None, 'dp'), may hold values from -0.109375 to 0.109375
- decay_rates: float32 [1, 8], replicated, may hold values from 0 to 0.034, as said below
- doc_lengths: int32 [16, 4], P('dp'), may hold values from 1 to 1024, 2048 in all within a row
- out_cotangent: bfloat16 [16, 2048, 1024], P('dp', 'seq'), may hold values from -6 to 6
Outputs:
- block_output: bfloat16 [16, 2048, 1024], P('dp', 'seq')
- input_gradient: float32 [16, 2048, 1024], P('dp', 'seq')
- mixer_gradient: float32 [1, 5, 1024, 1024], P(None, None, 'dp')
- channel_in_gradient: float32 [1, 2, 1024, 2816], P(None, None, 'dp')
- channel_out_gradient: float32 [1, 2816, 1024], P(None, 'dp')
Inputs may be any that keep to these rules, and one draw needn't show every extreme that they name: `decay_rates`: positive decay rates. `doc_lengths`: each row's 4 lengths add up to 2048.
All inputs are finite; a program needn't handle non-finite values.
Results may differ from a plain program's by a relative error of at most 0.02.
Values may be sent and summed in bfloat16 or wider, within the bound.
No kernel may reach another device: no remote copies, remote signals or barrier semaphores. Data moves between devices by JAX's collectives and lax.ppermute only.
A program may use at most 256 MiB of HBM per device.

v0:
```python
import jax
import jax.numpy as jnp
from jax import lax
from jax.sharding import PartitionSpec as P

EPS = 1e-06
FULL_PRECISION = lax.Precision.HIGHEST


def passed_along(value, axis, steps):
    count = lax.axis_size(axis)
    leading, last = (max(0, -steps), min(count, count - steps))
    return lax.ppermute(value, axis, [(source, source + steps) for source in range(leading, last)])


def product(left, right):
    return jnp.dot(left, right, preferred_element_type=jnp.float32)


def rms_norm(value_rows):
    factor = lax.rsqrt(jnp.mean(value_rows * value_rows, axis=-1, keepdims=True) + EPS)
    return (value_rows * factor, factor)


def norm_back(value_rows, factor, upstream):
    features = value_rows.shape[-1]
    inner_sum = jnp.sum(upstream * value_rows, axis=-1, keepdims=True)
    return factor * upstream - factor * factor * factor / features * value_rows * inner_sum


def swish_slope(value_rows):
    sigmoid_part = jax.nn.sigmoid(value_rows)
    return sigmoid_part * (1.0 + value_rows * (1.0 - sigmoid_part))


def doc_index(doc_ends, places):
    compare = places[None, :, None] >= doc_ends[:, None, :]
    return jnp.sum(compare.astype(jnp.int32), axis=-1, dtype=jnp.int32)


def decay_tables(rates, doc_ends, start, count):
    float_kind = rates.dtype
    offsets = jnp.arange(count, dtype=jnp.int32)
    start = jnp.asarray(start, dtype=jnp.int32)
    doc_here = doc_index(doc_ends, start + offsets)
    before_place = jnp.full((1,), -1, dtype=jnp.int32) + start
    doc_before = doc_index(doc_ends, before_place)[:, 0]
    doc_last = doc_here[:, count - 1]
    distance = jnp.maximum(offsets[:, None] - offsets[None, :], 0).astype(float_kind)
    causal = offsets[:, None] >= offsets[None, :]
    linked = causal[None] & (doc_here[:, :, None] == doc_here[:, None, :])
    intra_vals = jnp.exp(-rates[None, :, None, None] * distance[None, None])
    intra = jnp.where(linked[:, None], intra_vals, jnp.zeros_like(intra_vals))
    ahead = (offsets + 1).astype(float_kind)
    behind = (count - 1 - offsets).astype(float_kind)
    entry_vals = jnp.exp(-rates[None, None, :] * ahead[None, :, None])
    entry = jnp.where(
        (doc_here == doc_before[:, None])[:, :, None], entry_vals, jnp.zeros_like(entry_vals)
    )
    leaving_vals = jnp.exp(-rates[None, None, :] * behind[None, :, None])
    leaving = jnp.where(
        (doc_here == doc_last[:, None])[:, :, None], leaving_vals, jnp.zeros_like(leaving_vals)
    )
    length_value = jnp.asarray(count, dtype=float_kind)
    passing_vals = jnp.exp(-rates * length_value)[None, :] + jnp.zeros(
        (doc_last.shape[0], 1), float_kind
    )
    passing = jnp.where(
        (doc_last == doc_before)[:, None], passing_vals, jnp.zeros_like(passing_vals)
    )
    return (intra, entry, leaving, passing)


def block_out(per_head_queries, per_head_keys, per_head_values, tables, state_in):
    scores = (
        jnp.einsum("rthd,rshd->rhts", per_head_queries, per_head_keys, precision=FULL_PRECISION)
        * tables[0]
    )
    local_part = jnp.einsum("rhts,rshe->rthe", scores, per_head_values, precision=FULL_PRECISION)
    carried = (
        jnp.einsum("rthd,rhde->rthe", per_head_queries, state_in, precision=FULL_PRECISION)
        * tables[1][..., None]
    )
    return local_part + carried


def block_state(per_head_keys, per_head_values, tables):
    return jnp.einsum(
        "rshd,rshe->rhde",
        per_head_keys * tables[2][..., None],
        per_head_values,
        precision=FULL_PRECISION,
    )


def block_back(
    per_head_queries, per_head_keys, per_head_values, upstream, tables, state_in, state_grad
):
    intra, entry, leaving, passing = tables
    scores = (
        jnp.einsum("rthd,rshd->rhts", per_head_queries, per_head_keys, precision=FULL_PRECISION)
        * intra
    )
    score_grad = (
        jnp.einsum("rthe,rshe->rhts", upstream, per_head_values, precision=FULL_PRECISION) * intra
    )
    query_grad = jnp.einsum("rhts,rshd->rthd", score_grad, per_head_keys, precision=FULL_PRECISION)
    query_grad = (
        query_grad
        + jnp.einsum("rthe,rhde->rthd", upstream, state_in, precision=FULL_PRECISION)
        * entry[..., None]
    )
    key_grad = jnp.einsum("rhts,rthd->rshd", score_grad, per_head_queries, precision=FULL_PRECISION)
    key_grad = (
        key_grad
        + jnp.einsum("rshe,rhde->rshd", per_head_values, state_grad, precision=FULL_PRECISION)
        * leaving[..., None]
    )
    value_grad = jnp.einsum("rhts,rthe->rshe", scores, upstream, precision=FULL_PRECISION)
    value_grad = (
        value_grad
        + jnp.einsum("rshd,rhde->rshe", per_head_keys, state_grad, precision=FULL_PRECISION)
        * leaving[..., None]
    )
    return (query_grad, key_grad, value_grad)


def carry_forward(passing, local_state):

    def step_forward(turn_index, incoming):
        outgoing = passing[..., None, None] * incoming + local_state
        return passed_along(outgoing.astype(jnp.bfloat16), "seq", 1).astype(outgoing.dtype)

    return lax.fori_loop(0, lax.axis_size("seq") - 1, step_forward, jnp.zeros_like(local_state))


def carry_backward(passing, local_grad):

    def retreat(turn_index, incoming):
        outgoing = passing[..., None, None] * incoming + local_grad
        return passed_along(outgoing.astype(jnp.bfloat16), "seq", -1).astype(outgoing.dtype)

    return lax.fori_loop(0, lax.axis_size("seq") - 1, retreat, jnp.zeros_like(local_grad))


def reduce_grads(terms):
    pieces = (
        lax.psum_scatter(
            terms[0].astype(jnp.bfloat16), "dp", scatter_dimension=1, tiled=True
        ).astype(jnp.float32),
        lax.psum_scatter(
            terms[1].astype(jnp.bfloat16), "dp", scatter_dimension=0, tiled=True
        ).astype(jnp.float32),
        lax.psum_scatter(
            terms[2].astype(jnp.bfloat16), "dp", scatter_dimension=1, tiled=True
        ).astype(jnp.float32),
        lax.psum_scatter(
            terms[3].astype(jnp.bfloat16), "dp", scatter_dimension=0, tiled=True
        ).astype(jnp.float32),
    )
    return (
        lax.psum(pieces[0].astype(jnp.bfloat16), "seq").astype(jnp.float32),
        lax.psum(pieces[1].astype(jnp.bfloat16), "seq").astype(jnp.float32),
        lax.psum(pieces[2].astype(jnp.bfloat16), "seq").astype(jnp.float32),
        lax.psum(pieces[3].astype(jnp.bfloat16), "seq").astype(jnp.float32),
    )


def local(
    hidden_in,
    mixer_weights,
    channel_in_weights,
    channel_out_weights,
    decay_rates,
    doc_lengths,
    out_cotangent,
):
    rows, tokens, features = hidden_in.shape
    layers = mixer_weights.shape[0]
    heads = decay_rates.shape[1]
    head_dim = features // heads
    count = rows * tokens
    head_shape = (rows, tokens, heads, head_dim)
    start = lax.axis_index("seq") * jnp.asarray(tokens, dtype=jnp.int32)
    doc_ends = jnp.cumsum(doc_lengths, axis=1, dtype=jnp.int32)
    resid = hidden_in.astype(jnp.float32).reshape(count, features)
    layer_index = 0
    gathered = (
        mixer_weights[layer_index].astype(jnp.bfloat16),
        channel_in_weights[layer_index].astype(jnp.bfloat16),
        channel_out_weights[layer_index].astype(jnp.bfloat16),
    )
    mixer_full = lax.all_gather(gathered[0], "dp", axis=1, tiled=True)
    channel_full = lax.all_gather(gathered[1], "dp", axis=1, tiled=True)
    down_full = lax.all_gather(gathered[2], "dp", axis=0, tiled=True)
    normed, factor_in = rms_norm(resid)
    normed_low = normed.astype(jnp.bfloat16)
    projected = jnp.einsum(
        "nd,kde->kne", normed_low, mixer_full[:4], preferred_element_type=jnp.float32
    )
    query_pre = projected[0]
    key_pre = projected[1]
    value_pre = projected[2]
    gate_pre = projected[3]
    per_head_queries = (query_pre * jax.nn.sigmoid(query_pre)).reshape(head_shape)
    per_head_keys = (key_pre * jax.nn.sigmoid(key_pre)).reshape(head_shape)
    per_head_values = value_pre.reshape(head_shape)
    tables = decay_tables(decay_rates[layer_index], doc_ends, start, tokens)
    local_state = block_state(per_head_keys, per_head_values, tables)
    state_in = carry_forward(tables[3], local_state)
    mixed = block_out(per_head_queries, per_head_keys, per_head_values, tables, state_in).reshape(
        count, features
    )
    mixed_norm, factor_mix = rms_norm(mixed)
    gated = (mixed_norm * gate_pre).astype(jnp.bfloat16)
    after_mixer = resid + product(gated, mixer_full[4])
    normed_two, factor_two = rms_norm(after_mixer)
    normed_two_low = normed_two.astype(jnp.bfloat16)
    pair = jnp.einsum(
        "nd,kdf->knf", normed_two_low, channel_full, preferred_element_type=jnp.float32
    )
    glu = (pair[0] * pair[1]).astype(jnp.bfloat16)
    saved = [
        (
            mixer_full,
            channel_full,
            down_full,
            resid,
            factor_in,
            normed_low,
            query_pre,
            key_pre,
            gate_pre,
            per_head_queries,
            per_head_keys,
            per_head_values,
            tables,
            state_in,
            mixed,
            mixed_norm,
            factor_mix,
            gated,
            after_mixer,
            factor_two,
            normed_two_low,
            pair,
            glu,
        )
    ]
    resid = after_mixer + product(glu, down_full)
    block_output = resid.astype(jnp.bfloat16).reshape(rows, tokens, features)
    upstream = out_cotangent.astype(jnp.float32).reshape(count, features)
    mixer_list = []
    channel_list = []
    down_list = []
    for layer_index in reversed(range(layers)):
        (
            mixer_full,
            channel_full,
            down_full,
            resid_in,
            factor_in,
            normed_low,
            query_pre,
            key_pre,
            gate_pre,
            per_head_queries,
            per_head_keys,
            per_head_values,
            tables,
            state_in,
            mixed,
            mixed_norm,
            factor_mix,
            gated,
            after_mixer,
            factor_two,
            normed_two_low,
            pair,
            glu,
        ) = saved[layer_index]
        branch_low = upstream.astype(jnp.bfloat16)
        down_term = jnp.einsum("nf,nd->fd", glu, branch_low, preferred_element_type=jnp.float32)
        glu_grad = (
            jnp.einsum("nd,fd->nf", branch_low, down_full, preferred_element_type=jnp.float32)
            .astype(jnp.bfloat16)
            .astype(jnp.float32)
        )
        pair_grad = jnp.stack([glu_grad * pair[1], glu_grad * pair[0]]).astype(jnp.bfloat16)
        channel_term = jnp.einsum(
            "nd,knf->kdf", normed_two_low, pair_grad, preferred_element_type=jnp.float32
        )
        two_grad = jnp.einsum(
            "knf,kdf->nd", pair_grad, channel_full, preferred_element_type=jnp.float32
        )
        upstream_mid = upstream + norm_back(after_mixer, factor_two, two_grad)
        mixer_low = upstream_mid.astype(jnp.bfloat16)
        out_term = jnp.einsum("nd,ne->de", gated, mixer_low, preferred_element_type=jnp.float32)
        gated_grad = (
            jnp.einsum("ne,de->nd", mixer_low, mixer_full[4], preferred_element_type=jnp.float32)
            .astype(jnp.bfloat16)
            .astype(jnp.float32)
        )
        gate_grad = gated_grad * mixed_norm
        mixed_grad = norm_back(mixed, factor_mix, gated_grad * gate_pre).reshape(head_shape)
        local_grad = jnp.einsum(
            "rthd,rthe->rhde",
            per_head_queries * tables[1][..., None],
            mixed_grad,
            precision=FULL_PRECISION,
        )
        state_grad = carry_backward(tables[3], local_grad)
        query_grad, key_grad, value_grad = block_back(
            per_head_queries,
            per_head_keys,
            per_head_values,
            mixed_grad,
            tables,
            state_in,
            state_grad,
        )
        proj_grad = jnp.stack(
            [
                query_grad.reshape(count, features) * swish_slope(query_pre),
                key_grad.reshape(count, features) * swish_slope(key_pre),
                value_grad.reshape(count, features),
                gate_grad,
            ]
        ).astype(jnp.bfloat16)
        four_term = jnp.einsum(
            "nd,kne->kde", normed_low, proj_grad, preferred_element_type=jnp.float32
        )
        one_grad = jnp.einsum(
            "kne,kde->nd", proj_grad, mixer_full[:4], preferred_element_type=jnp.float32
        )
        upstream = upstream_mid + norm_back(resid_in, factor_in, one_grad)
        summed = reduce_grads((four_term, out_term, channel_term, down_term))
        mixer_list.append(jnp.concatenate([summed[0], summed[1][None]], axis=0))
        channel_list.append(summed[2])
        down_list.append(summed[3])
    mixer_gradient = jnp.stack(mixer_list[::-1])
    channel_in_gradient = jnp.stack(channel_list[::-1])
    channel_out_gradient = jnp.stack(down_list[::-1])
    input_gradient = upstream.reshape(rows, tokens, features)
    return (block_output, input_gradient, mixer_gradient, channel_in_gradient, channel_out_gradient)


def solution(mesh):
    in_specs = (
        P("dp", "seq", None),
        P(None, None, "dp", None),
        P(None, None, "dp", None),
        P(None, "dp", None),
        P(),
        P("dp", None),
        P("dp", "seq", None),
    )
    out_specs = (
        P("dp", "seq", None),
        P("dp", "seq", None),
        P(None, None, "dp", None),
        P(None, None, "dp", None),
        P(None, "dp", None),
    )
    return jax.shard_map(local, mesh=mesh, in_specs=in_specs, out_specs=out_specs, check_vma=False)
```

profile of v0, /device:TPU:0, one launch (start us, length us, event | category | flops | bytes accessed | tf_op | source)
XLA Modules:
  0.0 966.9 jit_solution(12912789637610193381)
XLA Ops:
  26.6 51.9 %all-gather.7.cloned.1.call-done = bf16[1,5,1024,1024]{2,3,1,0:T(8,128)(2,1)} async-done(((bf16[1,5,128,1024]{2,3,1,0:T(8,128)(2,1)}), bf16[1,5,1024,1024]{2,3,1,0:T(8,128)(2,1)}) %all-gather.7.cloned.1.call-update) | async-done | bytes 10485776 | tf_op jit(solution)/shard_map/all_gather | solution.py:193
  78.5 16.3 %convolution_bitcast_fusion = f32[4,1024,1024]{1,2,0:T(8,128)} fusion(bf16[1,5,1024,1024]{2,3,1,0:T(8,128)(2,1)} %all-gather.7.cloned.1.call-done, bf16[1024,1024]{1,0:T(8,128)(2,1)} %fusion.65), kind=kOutput, calls=%fused_computation.30 | convolution fusion | flops 8589934592 | bytes 27262976 | tf_op jit(solution)/shard_map/nd,kde->kne/dot_general | solution.py:198
  94.7 10.2 %fusion.120 = (f32[1,1024,1024]{1,2,0:T(8,128)}, f32[1,1024,1024]{1,2,0:T(8,128)}, f32[1,1024,1024]{1,2,0:T(8,128)}) fusion(f32[4,1024,1024]{1,2,0:T(8,128)} %convolution_bitcast_fusion), kind=kLoop, calls=%fused_computation.166 | loop fusion | bytes 25165824 | tf_op jit(solution)/shard_map/slice | solution.py:201
  140.8 48.7 %while.22 = (s32[]{:T(128)}, f32[2,8,128,128]{3,2,1,0:T(8,128)S(1)}, f32[2,8,128,128]{3,2,1,0:T(8,128)S(1)}, f32[8]{0:T(128)S(1)}, pred[2]{0:T(512)(128)(4,1)S(1)}, /*index=5*/s32[]{:T(128)}, s32[]{:T(128)}) while((s32[]{:T(128)}, f32[2,8,128,128]{3,2,1,0:T(8,128)S(1)}, f32[2,8,128,128]{3,2,1,0:T(8,128)S(1)}, f32[8]{0:T(128)S(1)}, ...), condition=%wide.region_5.6_spmd.clone, body=%wide.region_4.5_spmd.clone.sunk | while | flops 1310739 | bytes 6291745 | solution.py:134
  145.3 11.9 %collective-permute-done = bf16[2,8,128,128]{3,2,1,0:T(8,128)(2,1)S(1)} collective-permute-done((bf16[2,8,128,128]{3,2,1,0:T(8,128)(2,1)}, bf16[2,8,128,128]{3,2,1,0:T(8,128)(2,1)S(1)}, u32[]{:S(2)}, u32[]{:S(2)}) %collective-permute-start) | collective-permute-done | bytes 524320 | tf_op jit(solution)/shard_map/while/body/eval_jaxpr/ppermute | solution.py:13
  162.7 11.1 %collective-permute-done = bf16[2,8,128,128]{3,2,1,0:T(8,128)(2,1)S(1)} collective-permute-done((bf16[2,8,128,128]{3,2,1,0:T(8,128)(2,1)}, bf16[2,8,128,128]{3,2,1,0:T(8,128)(2,1)S(1)}, u32[]{:S(2)}, u32[]{:S(2)}) %collective-permute-start) | collective-permute-done | bytes 524320 | tf_op jit(solution)/shard_map/while/body/eval_jaxpr/ppermute | solution.py:13
  179.2 10.1 %collective-permute-done = bf16[2,8,128,128]{3,2,1,0:T(8,128)(2,1)S(1)} collective-permute-done((bf16[2,8,128,128]{3,2,1,0:T(8,128)(2,1)}, bf16[2,8,128,128]{3,2,1,0:T(8,128)(2,1)S(1)}, u32[]{:S(2)}, u32[]{:S(2)}) %collective-permute-start) | collective-permute-done | bytes 524320 | tf_op jit(solution)/shard_map/while/body/eval_jaxpr/ppermute | solution.py:13
  198.8 17.2 %fusion.118 = f32[2,8,512,512]{3,2,1,0:T(8,128)} fusion(f32[2,512,8,128]{1,0,3,2:T(2,128)S(1)} %copy-done.14, f32[2,512,8,128]{1,0,3,2:T(2,128)S(1)} %copy-done.13), kind=kOutput, calls=%fused_computation.164 | convolution fusion | flops 6450839552 | bytes 25165824 | tf_op jit(solution)/shard_map/rthd,rshd->rhts/dot_general | solution.py:76
  216.0 23.7 %multiply_reduce_fusion.2 = (f32[2,512]{1,0:T(2,128)S(1)}, f32[2,512,8,128]{1,3,2,0:T(8,128)}) fusion(f32[2,512,8]{1,2,0:T(8,128)S(1)} %get-tuple-element.166, f32[2,8,128,512]{3,2,1,0:T(8,128)} %fusion.119, f32[2,512,8,128]{3,1,2,0:T(8,128)} %copy.119, f32[2,8,512,512]{3,2,1,0:T(8,128)} %fusion.118, f32[8,512,512]{2,1,0:T(8,128)} %multiply_exponential_fusion, ...), kind=kOutput, calls=%fused_computation.99 | convolution fusion | flops 6455032832 | bytes 38309888 | tf_op jit(solution)/shard_map/rhts,rshe->rthe/dot_general | solution.py:79
  267.0 20.9 %fusion.19 = f32[2,1024,2816]{2,1,0:T(8,128)} fusion(bf16[1,2,1024,2816]{3,2,1,0:T(8,128)(2,1)} %all-gather.9.cloned.1.call-done, f32[1024,1024]{1,0:T(8,128)} %get-tuple-element.159, f32[1024]{0:T(1024)S(1)} %get-tuple-element.149), kind=kOutput, calls=%fused_computation.29 | convolution fusion | flops 11813257216 | bytes 38801408 | tf_op jit(solution)/shard_map/nd,kdf->knf/dot_general | solution.py:219
  287.9 14.9 %fusion.41 = (bf16[1,1024,2816]{2,1,0:T(8,128)(2,1)}, bf16[1,1024,2816]{2,1,0:T(8,128)(2,1)}) fusion(f32[2,1024,2816]{2,1,0:T(8,128)} %fusion.19, bf16[1024,1024]{1,0:T(8,128)(2,1)S(1)} %bitcast.231, bf16[1,2816,1024]{2,1,0:T(8,128)(2,1)} %all-gather.11.cloned.1.call-done), kind=kOutput, calls=%fused_computation.52 | convolution fusion | flops 5922881536 | bytes 42467328 | tf_op jit(solution)/shard_map/nd,fd->nf/dot_general | solution.py:285
  302.9 20.3 %fusion.62 = (f32[1024]{0:T(1024)S(1)}, f32[1024,1024,1]{1,0,2:T(8,128)}) fusion(f32[1024,1024]{1,0:T(8,128)} %get-tuple-element.159, bf16[1,2,1024,2816]{3,2,1,0:T(8,128)(2,1)} %all-gather.9.cloned.1.call-done, bf16[1,1024,2816]{2,1,0:T(8,128)(2,1)} %get-tuple-element.140, bf16[1,1024,2816]{2,1,0:T(8,128)(2,1)} %get-tuple-element.139), kind=kOutput, calls=%fused_computation.79 | convolution fusion | flops 11819023360 | bytes 31461376 | tf_op jit(solution)/shard_map/knf,kdf->nd/dot_general | solution.py:293
  348.0 19.9 %fusion.8 = f32[2,8,128,512]{3,2,1,0:T(8,128)} fusion(f32[2,8,512,512]{3,2,1,0:T(8,128)} %fusion.118, f32[8,512,512]{2,1,0:T(8,128)} %multiply_exponential_fusion, pred[2,512,512]{2,1,0:T(8,128)(4,1)S(1)} %compare_and_fusion, f32[2,512,8,128]{1,0,3,2:T(2,128)} %reshape.344), kind=kOutput, calls=%fused_computation.12 | convolution fusion | flops 6450839552 | bytes 34078720 | tf_op jit(solution)/shard_map/rhts,rthe->rshe/dot_general | solution.py:119
  376.8 16.0 %fusion.74 = f32[2,8,512,512]{3,2,1,0:T(8,128)} fusion(f32[2,512,8,128]{3,1,2,0:T(8,128)S(1)} %copy-done.5, f32[2,512,8,128]{1,0,3,2:T(2,128)S(1)} %copy-done.6), kind=kOutput, calls=%fused_computation.107 | convolution fusion | flops 6442450944 | bytes 25165824 | tf_op jit(solution)/shard_map/rthe,rshe->rhts/dot_general | solution.py:105
  398.8 43.1 %while.23 = (s32[]{:T(128)}, f32[2,8,128,128]{3,2,1,0:T(8,128)S(1)}, f32[2,8,128,128]{3,2,1,0:T(8,128)S(1)}, f32[8]{0:T(128)S(1)}, pred[2]{0:T(512)(128)(4,1)S(1)}, /*index=5*/s32[]{:T(128)}, s32[]{:T(128)}) while((s32[]{:T(128)}, f32[2,8,128,128]{3,2,1,0:T(8,128)S(1)}, f32[2,8,128,128]{3,2,1,0:T(8,128)S(1)}, f32[8]{0:T(128)S(1)}, ...), condition=%wide.region_11.12_spmd.clone, body=%wide.region_10.11_spmd.clone.sunk | while | flops 1310739 | bytes 6291745 | solution.py:143
  401.1 13.0 %collective-permute-done.1 = bf16[2,8,128,128]{3,2,1,0:T(8,128)(2,1)S(1)} collective-permute-done((bf16[2,8,128,128]{3,2,1,0:T(8,128)(2,1)}, bf16[2,8,128,128]{3,2,1,0:T(8,128)(2,1)S(1)}, u32[]{:S(2)}, u32[]{:S(2)}) %collective-permute-start.1) | collective-permute-done | bytes 524320 | tf_op jit(solution)/shard_map/while/body/eval_jaxpr/ppermute | solution.py:13
  416.6 11.7 %collective-permute-done.1 = bf16[2,8,128,128]{3,2,1,0:T(8,128)(2,1)S(1)} collective-permute-done((bf16[2,8,128,128]{3,2,1,0:T(8,128)(2,1)}, bf16[2,8,128,128]{3,2,1,0:T(8,128)(2,1)S(1)}, u32[]{:S(2)}, u32[]{:S(2)}) %collective-permute-start.1) | collective-permute-done | bytes 524320 | tf_op jit(solution)/shard_map/while/body/eval_jaxpr/ppermute | solution.py:13
  430.7 10.8 %collective-permute-done.1 = bf16[2,8,128,128]{3,2,1,0:T(8,128)(2,1)S(1)} collective-permute-done((bf16[2,8,128,128]{3,2,1,0:T(8,128)(2,1)}, bf16[2,8,128,128]{3,2,1,0:T(8,128)(2,1)S(1)}, u32[]{:S(2)}, u32[]{:S(2)}) %collective-permute-start.1) | collective-permute-done | bytes 524320 | tf_op jit(solution)/shard_map/while/body/eval_jaxpr/ppermute | solution.py:13
  459.8 28.1 %fusion.11 = f32[2,8,128,512]{3,2,1,0:T(8,128)} fusion(f32[2,8,512,512]{3,2,1,0:T(8,128)} %fusion.74, f32[8,512,512]{2,1,0:T(8,128)} %multiply_exponential_fusion, pred[2,512,512]{2,1,0:T(8,128)(4,1)S(1)} %compare_and_fusion, f32[2,512,8,128]{1,0,3,2:T(2,128)} %squeeze.13), kind=kOutput, calls=%fused_computation.15 | convolution fusion | flops 6455033856 | bytes 34078720 | tf_op jit(solution)/shard_map/rhts,rshd->rthd/dot_general | solution.py:107
  508.2 21.7 %fusion.57 = f32[2,512,8,128]{1,3,2,0:T(8,128)} fusion(f32[2,8,128,512]{3,2,1,0:T(8,128)} %fusion.123, f32[2,8,512,512]{3,2,1,0:T(8,128)} %fusion.74, f32[8,512,512]{2,1,0:T(8,128)} %multiply_exponential_fusion, pred[2,512,512]{2,1,0:T(8,128)(4,1)S(1)} %compare_and_fusion, f32[2,512,8]{1,2,0:T(8,128)S(1)} %copy-done.28, f32[2,512,8,128]{1,0,3,2:T(2,128)} %squeeze.12), kind=kOutput, calls=%fused_computation.70 | convolution fusion | flops 6457131008 | bytes 38305792 | tf_op jit(solution)/shard_map/rhts,rthd->rshd/dot_general | solution.py:113
  554.5 11.0 %convert_bitcast_fusion.1 = bf16[4,1024,1024]{1,2,0:T(8,128)(2,1)} fusion(bf16[1024,1024]{1,0:T(8,128)(2,1)S(1)} %copy-done.22, bf16[1,1024,1024]{1,2,0:T(8,128)(2,1)S(1)} %copy-done.19, bf16[1,1024,1024]{1,2,0:T(8,128)(2,1)S(1)} %copy-done.23, bf16[1,1024,1024]{1,2,0:T(8,128)(2,1)S(1)} %get-tuple-element.142, bf16[1,1024,1024]{1,2,0:T(8,128)(2,1)S(1)} %get-tuple-element.141), kind=kOutput, calls=%fused_computation.33 | convolution fusion | flops 8606711808 | bytes 18874368 | tf_op jit(solution)/shard_map/nd,kne->kde/dot_general | solution.py:330
  565.5 15.0 %copy.151 = bf16[4,1024,1024]{2,0,1:T(4,128)(2,1)} copy(bf16[4,1024,1024]{1,2,0:T(8,128)(2,1)} %convert_bitcast_fusion.1) | data formatting | bytes 16777216
  580.5 12.3 %copy.160 = bf16[128,8,4,1024]{3,1,2,0:T(8,128)(2,1)} copy(bf16[128,8,4,1024]{3,2,1,0:T(4,128)(2,1)} %bitcast.226) | data formatting | bytes 16777216
  592.8 19.1 %convert_bitcast_fusion = bf16[2,1024,2816]{1,2,0:T(8,128)(2,1)} fusion(bf16[1,1024,2816]{2,1,0:T(8,128)(2,1)} %get-tuple-element.140, bf16[1,1024,2816]{2,1,0:T(8,128)(2,1)} %get-tuple-element.139, f32[1024,1024]{1,0:T(8,128)} %get-tuple-element.159, f32[1024]{0:T(1024)S(1)} %get-tuple-element.149), kind=kOutput, calls=%fused_computation.28 | convolution fusion | flops 11824791552 | bytes 27267072 | tf_op jit(solution)/shard_map/nd,knf->kdf/dot_general | solution.py:290
  611.9 29.1 %copy.155 = bf16[2,1024,2816]{2,0,1:T(2,128)(2,1)} copy(bf16[2,1024,2816]{1,2,0:T(8,128)(2,1)} %convert_bitcast_fusion) | data formatting | bytes 23068672
  641.0 11.4 %copy.161 = bf16[128,8,2,2816]{3,1,2,0:T(8,128)(2,1)} copy(bf16[128,8,2,2816]{3,2,1,0:T(2,128)(2,1)} %bitcast.223) | data formatting | bytes 23068672
  654.0 15.9 %fusion.45 = bf16[2816,1024]{1,0:T(8,128)(2,1)} fusion(bf16[1024,1024]{1,0:T(8,128)(2,1)S(1)} %bitcast.232, f32[2,1024,2816]{2,1,0:T(8,128)} %fusion.19), kind=kOutput, calls=%fused_computation.56 | convolution fusion | flops 5914230784 | bytes 30932992 | tf_op jit(solution)/shard_map/nf,nd->fd/dot_general | solution.py:283
  676.2 76.9 %reduce-scatter.17.cloned.1.call-done = bf16[128,5632]{1,0:T(8,128)(2,1)} async-done(((bf16[1024,5632]{1,0:T(8,128)(2,1)}), bf16[128,5632]{1,0:T(8,128)(2,1)}) %reduce-scatter.17.cloned.1.call-update) | async-done | bytes 1441808
  759.6 56.0 %reduce-scatter.11.cloned.1.call-done = bf16[352,1024]{1,0:T(8,128)(2,1)} async-done(((bf16[2816,1024]{1,0:T(8,128)(2,1)}), bf16[352,1024]{1,0:T(8,128)(2,1)}) %reduce-scatter.11.cloned.1.call-update) | async-done | bytes 720912 | tf_op jit(solution)/shard_map/reduce_scatter | solution.py:157
  815.7 15.1 %fusion.54 = (f32[1024]{0:T(1024)S(1)}, f32[1024,1024,1]{1,0,2:T(8,128)S(1)}) fusion(bf16[2,512,1024]{2,1,0:T(8,128)(2,1)S(1)} %copy-done.12, bf16[1,5,1024,1024]{2,3,1,0:T(8,128)(2,1)} %all-gather.7.cloned.1.call-done, bf16[1,1024,1024]{1,2,0:T(8,128)(2,1)} %get-tuple-element.147, bf16[1,1024,1024]{1,2,0:T(8,128)(2,1)} %stack_reshape.4, ...), kind=kOutput, calls=%fused_computation.65 | convolution fusion | flops 8605662208 | bytes 23072768 | tf_op jit(solution)/shard_map/kne,kde->nd/dot_general | solution.py:333
  834.4 13.7 %add_convert_fusion = bf16[1024,1024]{1,0:T(8,128)(2,1)} fusion(f32[1024,1024]{1,0:T(8,128)S(1)} %copy-done.17, bf16[1,2816,1024]{2,1,0:T(8,128)(2,1)} %all-gather.11.cloned.1.call-done, f32[2,1024,2816]{2,1,0:T(8,128)} %fusion.19), kind=kOutput, calls=%fused_computation.95 | convolution fusion | flops 5913444352 | bytes 35127296 | tf_op jit(solution)/shard_map/dot_general | solution.py:17
  848.1 103.7 %all-reduce.3.cloned.1.call-done = (bf16[1,2,128,2816]{2,3,1,0:T(8,128)(2,1)}, bf16[1,128,1024]{1,2,0:T(8,128)(2,1)}, bf16[4,128,1024]{1,2,0:T(8,128)(2,1)}, bf16[1,352,1024]{2,1,0:T(8,128)(2,1)}) async-done(((bf16[1,2,128,2816]{2,3,1,0:T(8,128)(2,1)}, bf16[1,128,1024]{1,2,0:T(8,128)(2,1)}, bf16[4,128,1024]{1,2,0:T(8,128)(2,1)}, bf16[1,352,1024]{2,1,0:T(8,128)(2,1)}), (bf16[1,2,128,2816]{2,3,1,0:T(8,128)(2,1)}, ...) | async-done | bytes 3473424 | tf_op jit(solution)/shard_map/psum | solution.py:164
  (185 shorter events, 242.5 us)
Async XLA Ops:
  7.2 71.3 %all-gather.7.cloned.1.call-start = ((), (), s32[]{:S(2)}) async-start(), calls=%async_computation.5 | async-start | bytes 11796480 | tf_op jit(solution)/shard_map/all_gather | solution.py:193
  10.0 256.9 %all-gather.9.cloned.1.call-start = ((), (), s32[]{:S(2)}) async-start(), calls=%async_computation.6 | async-start | bytes 12976128 | tf_op jit(solution)/shard_map/all_gather | solution.py:194
  13.3 274.6 %all-gather.11.cloned.1.call-start = ((), (), s32[]{:S(2)}) async-start(), calls=%async_computation.7 | async-start | bytes 6488064 | tf_op jit(solution)/shard_map/all_gather | solution.py:195
  15.7 654.9 %reduce-scatter.15.cloned.1.call-start = ((), (), s32[]{:S(2)}) async-start(), calls=%async_computation.9 | async-start | bytes 2359296
  26.6 105.7 %copy-start.27 = (f32[2,512,8]{1,2,0:T(8,128)}, f32[2,512,8]{1,2,0:T(8,128)S(1)}, u32[]{:S(2)}) copy-start(f32[2,512,8]{1,2,0:T(8,128)S(1)} %get-tuple-element.167) | copy-start | bytes 98308
  141.9 15.3 %collective-permute-start = (bf16[2,8,128,128]{3,2,1,0:T(8,128)(2,1)}, bf16[2,8,128,128]{3,2,1,0:T(8,128)(2,1)S(1)}, u32[]{:S(2)}, u32[]{:S(2)}) collective-permute-start(bf16[2,8,128,128]{3,2,1,0:T(8,128)(2,1)} %fusion.136), channel_id=1, source_target_pairs={{0,8},{8,16},{16,24},{1,9},{9,17},{17,25},{2,10},{10,18},{18,26},{... | collective-permute-start | bytes 1572872 | tf_op jit(solution)/shard_map/while/body/eval_jaxpr/ppermute | solution.py:13
  158.4 15.4 %collective-permute-start = (bf16[2,8,128,128]{3,2,1,0:T(8,128)(2,1)}, bf16[2,8,128,128]{3,2,1,0:T(8,128)(2,1)S(1)}, u32[]{:S(2)}, u32[]{:S(2)}) collective-permute-start(bf16[2,8,128,128]{3,2,1,0:T(8,128)(2,1)} %fusion.136), channel_id=1, source_target_pairs={{0,8},{8,16},{16,24},{1,9},{9,17},{17,25},{2,10},{10,18},{18,26},{... | collective-permute-start | bytes 1572872 | tf_op jit(solution)/shard_map/while/body/eval_jaxpr/ppermute | solution.py:13
  174.9 14.5 %collective-permute-start = (bf16[2,8,128,128]{3,2,1,0:T(8,128)(2,1)}, bf16[2,8,128,128]{3,2,1,0:T(8,128)(2,1)S(1)}, u32[]{:S(2)}, u32[]{:S(2)}) collective-permute-start(bf16[2,8,128,128]{3,2,1,0:T(8,128)(2,1)} %fusion.136), channel_id=1, source_target_pairs={{0,8},{8,16},{16,24},{1,9},{9,17},{17,25},{2,10},{10,18},{18,26},{... | collective-permute-start | bytes 1572872 | tf_op jit(solution)/shard_map/while/body/eval_jaxpr/ppermute | solution.py:13
  189.5 9.2 copy-start.8
  189.5 9.2 copy-start.31
  189.5 9.2 copy-start.33
  189.5 9.2 copy-start.13
  189.5 9.2 copy-start.14
  267.0 20.9 %copy-start.24 = (bf16[2,512,1024]{2,1,0:T(8,128)(2,1)S(1)}, bf16[2,512,1024]{2,1,0:T(8,128)(2,1)}, u32[]{:S(2)}) copy-start(bf16[2,512,1024]{2,1,0:T(8,128)(2,1)} %param.17) | copy-start | bytes 6291460
  367.9 8.9 copy-start.5
  367.9 8.9 copy-start.6
  376.8 16.0 %copy-start.1 = (f32[128,8,2,512]{3,1,2,0:T(8,128)S(1)}, f32[128,8,2,512]{3,1,2,0:T(8,128)}, u32[]{:S(2)}) copy-start(f32[128,8,2,512]{3,1,2,0:T(8,128)} %copy.159) | copy-start | bytes 12582916
  376.8 16.0 %copy-start.3 = (f32[1024,1024]{1,0:T(8,128)S(1)}, f32[1024,1024]{1,0:T(8,128)}, u32[]{:S(2)}) copy-start(f32[1024,1024]{1,0:T(8,128)} %copy-done.2) | copy-start | bytes 12582916
  399.8 14.3 %collective-permute-start.1 = (bf16[2,8,128,128]{3,2,1,0:T(8,128)(2,1)}, bf16[2,8,128,128]{3,2,1,0:T(8,128)(2,1)S(1)}, u32[]{:S(2)}, u32[]{:S(2)}) collective-permute-start(bf16[2,8,128,128]{3,2,1,0:T(8,128)(2,1)} %fusion.137), channel_id=1, source_target_pairs={{8,0},{16,8},{24,16},{9,1},{17,9},{25,17},{10,2},{18,10},{26,18},{... | collective-permute-start | bytes 1572872 | tf_op jit(solution)/shard_map/while/body/eval_jaxpr/ppermute | solution.py:13
  415.3 13.0 %collective-permute-start.1 = (bf16[2,8,128,128]{3,2,1,0:T(8,128)(2,1)}, bf16[2,8,128,128]{3,2,1,0:T(8,128)(2,1)S(1)}, u32[]{:S(2)}, u32[]{:S(2)}) collective-permute-start(bf16[2,8,128,128]{3,2,1,0:T(8,128)(2,1)} %fusion.137), channel_id=1, source_target_pairs={{8,0},{16,8},{24,16},{9,1},{17,9},{25,17},{10,2},{18,10},{26,18},{... | collective-permute-start | bytes 1572872 | tf_op jit(solution)/shard_map/while/body/eval_jaxpr/ppermute | solution.py:13
  429.5 12.1 %collective-permute-start.1 = (bf16[2,8,128,128]{3,2,1,0:T(8,128)(2,1)}, bf16[2,8,128,128]{3,2,1,0:T(8,128)(2,1)S(1)}, u32[]{:S(2)}, u32[]{:S(2)}) collective-permute-start(bf16[2,8,128,128]{3,2,1,0:T(8,128)(2,1)} %fusion.137), channel_id=1, source_target_pairs={{8,0},{16,8},{24,16},{9,1},{17,9},{25,17},{10,2},{18,10},{26,18},{... | collective-permute-start | bytes 1572872 | tf_op jit(solution)/shard_map/while/body/eval_jaxpr/ppermute | solution.py:13
  441.9 8.1 copy-start.15
  459.8 28.1 %copy-start.9 = (f32[2,8,128,128]{3,2,1,0:T(8,128)S(1)}, f32[2,8,128,128]{3,2,1,0:T(8,128)}, u32[]{:S(2)}) copy-start(f32[2,8,128,128]{3,2,1,0:T(8,128)} %copy-done.8) | copy-start | bytes 3145732
  544.0 10.4 %copy-start.19 = (bf16[1,1024,1024]{1,2,0:T(8,128)(2,1)S(1)}, bf16[1,1024,1024]{1,2,0:T(8,128)(2,1)}, u32[]{:S(2)}) copy-start(bf16[1,1024,1024]{1,2,0:T(8,128)(2,1)} %get-tuple-element.147) | copy-start | bytes 6291460
  544.0 128.4 %reduce-scatter.13.cloned.1.call-start = ((), (), s32[]{:S(2)}) async-start(), calls=%async_computation.8 | async-start | bytes 9437184
  544.1 10.4 %copy-start.22 = (bf16[1024,1024]{1,0:T(8,128)(2,1)S(1)}, bf16[1024,1024]{1,0:T(8,128)(2,1)}, u32[]{:S(2)}) copy-start(bf16[1024,1024]{1,0:T(8,128)(2,1)} %fusion.65) | copy-start | bytes 6291460
  544.1 10.4 %copy-start.23 = (bf16[1,1024,1024]{1,2,0:T(8,128)(2,1)S(1)}, bf16[1,1024,1024]{1,2,0:T(8,128)(2,1)}, u32[]{:S(2)}) copy-start(bf16[1,1024,1024]{1,2,0:T(8,128)(2,1)} %stack_reshape.4) | copy-start | bytes 6291460
  592.7 160.4 %reduce-scatter.17.cloned.1.call-start = ((), (), s32[]{:S(2)}) async-start(), calls=%async_computation.10 | async-start | bytes 12976128
  652.4 163.2 %reduce-scatter.11.cloned.1.call-start = ((), (), s32[]{:S(2)}) async-start(), calls=%async_computation.4 | async-start | bytes 6488064 | tf_op jit(solution)/shard_map/reduce_scatter | solution.py:157
  670.0 281.8 %all-reduce.3.cloned.1.call-start = ((), (), s32[]{:S(2)}) async-start(), calls=%async_computation.11 | async-start | bytes 6946816 | tf_op jit(solution)/shard_map/psum | solution.py:164
  676.2 139.5 %copy-start.12 = (bf16[2,512,1024]{2,1,0:T(8,128)(2,1)S(1)}, bf16[2,512,1024]{2,1,0:T(8,128)(2,1)}, u32[]{:S(2)}) copy-start(bf16[2,512,1024]{2,1,0:T(8,128)(2,1)} %param.11) | copy-start | bytes 6291460
  815.7 15.1 %copy-start.4 = (f32[1024,1024]{1,0:T(8,128)S(1)}, f32[1024,1024]{1,0:T(8,128)}, u32[]{:S(2)}) copy-start(f32[1024,1024]{1,0:T(8,128)} %copy-done.2) | copy-start | bytes 12582916
  (19 other events, 87.1 us)
Sparse Core Ops, SparseCore 0:
  10.4 67.9 all-gather.6
  80.9 67.6 all-gather.8
  150.5 43.3 all-gather.10
  544.1 40.0 reduce-scatter.14
  592.9 70.0 reduce-scatter.12
  666.3 86.8 reduce-scatter.16
  756.6 59.0 reduce-scatter.10
  819.1 132.6 all-reduce.2
where the time goes:
time: 978 us; the launch traced here: 967 us
  waiting for transfers between devices  357 us (37%)
  matrix products  343 us (35%)
  local copies, waits for them, and re-layouts  187 us (19%)
  other arithmetic  47.8 us (5%)
  starting transfers between devices  16.2 us (2%)
  between operations  15.2 us (2%)
    psum x1, waiting for transfers between devices, reduce_grads(): lax.psum(pieces[2].astype(jnp.bfloat16), 'seq').astype(jnp.float32)  104 us
    unnamed x89, local copies, waits for them, and re-layouts  98 us
    unnamed x11, waiting for transfers between devices  77.1 us
    ppermute x6, waiting for transfers between devices, passed_along(): lax.ppermute(value, axis, [(source, source + steps) for source in range(l...  68.6 us
    reduce_scatter x1, waiting for transfers between devices, reduce_grads(): lax.psum_scatter(terms[3].astype(jnp.bfloat16), 'dp', scatter_dimension=0...  56 us
    all_gather x1, waiting for transfers between devices, local(): mixer_full = lax.all_gather(gathered[0], 'dp', axis=1, tiled=True)  51.9 us
    dot_general x1, matrix products, block_back(): jnp.einsum('rhts,rshd->rthd', score_grad, per_head_keys, precision=FULL_P...  28.1 us
    dot_general x1, matrix products, block_out(): jnp.einsum('rhts,rshe->rthe', scores, per_head_values, precision=FULL_PRE...  23.7 us
  transfers between devices with their start and end apart: 14, of which 10 were waited for; matrix products, arithmetic and copies ran while one was open for 36% of the time, Pallas kernels for 0%

commit v1 on v0

--- a/solution.py
+++ b/solution.py
@@ -190,7 +190,12 @@
         channel_in_weights[layer_index].astype(jnp.bfloat16),
         channel_out_weights[layer_index].astype(jnp.bfloat16),
     )
-    mixer_full = lax.all_gather(gathered[0], "dp", axis=1, tiled=True)
+    ring = [gathered[0]]
+    for hop in range(7):
+        ring.append(lax.ppermute(ring[-1], "dp", [(dev, (dev + 1) % 8) for dev in range(8)]))
+    mixer_full = jnp.roll(
+        jnp.concatenate(ring[::-1], axis=1), (lax.axis_index("dp") + 1) * ring[0].shape[1], axis=1
+    )
     channel_full = lax.all_gather(gathered[1], "dp", axis=1, tiled=True)
     down_full = lax.all_gather(gathered[2], "dp", axis=0, tiled=True)
     normed, factor_in = rms_norm(resid)

time: 978 us -> 1140 us (1.17)
  waiting for transfers between devices: 357 us -> 464 us
  local copies, waits for them, and re-layouts: 187 us -> 221 us
  starting transfers between devices: 16.2 us -> 32.9 us
    ppermute x0 -> x7, waiting for transfers between devices: none -> 165 us  [local(): lax.ppermute(ring[-1], 'dp', [(dev, (dev + 1) % 8) for dev in range(8)])]
    all_gather x1 -> x0, waiting for transfers between devices: 51.9 us -> none  [local(): mixer_full = lax.all_gather(gathered[0], 'dp', axis=1, tiled=True)]
    unnamed x89 -> x122, local copies, waits for them, and re-layouts: 98 us -> 131 us
    unnamed x11 -> x10, waiting for transfers between devices: 77.1 us -> 77.2 us
  transfers between devices with their start and end apart: 14 -> 20, of which waited for: 10 -> 16; matrix products, arithmetic and copies ran while one was open for 36% -> 34% of each run, Pallas kernels for 0% -> 0%
where the time goes in v1:
time: 1140 us; the launch traced here: 1130 us
  waiting for transfers between devices  464 us (41%)
  matrix products  342 us (30%)
  local copies, waits for them, and re-layouts  221 us (19%)
  other arithmetic  51.8 us (5%)
  starting transfers between devices  32.9 us (3%)
  between operations  15.2 us (1%)
    ppermute x7, waiting for transfers between devices, local(): lax.ppermute(ring[-1], 'dp', [(dev, (dev + 1) % 8) for dev in range(8)])  165 us
    unnamed x122, local copies, waits for them, and re-layouts  131 us
    psum x1, waiting for transfers between devices, reduce_grads(): lax.psum(pieces[2].astype(jnp.bfloat16), 'seq').astype(jnp.float32)  105 us
    unnamed x10, waiting for transfers between devices  77.2 us
    ppermute x6, waiting for transfers between devices, passed_along(): lax.ppermute(value, axis, [(source, source + steps) for source in range(l...  61.3 us
    reduce_scatter x1, waiting for transfers between devices, reduce_grads(): lax.psum_scatter(terms[3].astype(jnp.bfloat16), 'dp', scatter_dimension=0...  55.9 us
    dot_general x1, matrix products, block_back(): jnp.einsum('rhts,rshd->rthd', score_grad, per_head_keys, precision=FULL_P...  27.9 us
    ppermute x6, starting transfers between devices, passed_along(): lax.ppermute(value, axis, [(source, source + steps) for source in range(l...  27.2 us
  transfers between devices with their start and end apart: 20, of which 16 were waited for; matrix products, arithmetic and copies ran while one was open for 34% of the time, Pallas kernels for 0%

profile of v1, /device:TPU:0, one launch (start us, length us, event | category | flops | bytes accessed | tf_op | source)
XLA Modules:
  0.0 1128.2 jit_solution(1122919101500040450)
XLA Ops:
  13.8 32.4 %collective-permute-done.2 = bf16[5,128,1024]{1,2,0:T(8,128)(2,1)S(1)} collective-permute-done((bf16[5,128,1024]{1,2,0:T(8,128)(2,1)}, bf16[5,128,1024]{1,2,0:T(8,128)(2,1)S(1)}, u32[]{:S(2)}, u32[]{:S(2)}) %collective-permute-start.2) | collective-permute-done | bytes 1310752 | tf_op jit(solution)/shard_map/ppermute | solution.py:195
  47.7 35.5 %collective-permute-done.3 = bf16[5,128,1024]{1,2,0:T(8,128)(2,1)S(1)} collective-permute-done((bf16[5,128,1024]{1,2,0:T(8,128)(2,1)S(1)}, bf16[5,128,1024]{1,2,0:T(8,128)(2,1)S(1)}, u32[]{:S(2)}, u32[]{:S(2)}) %collective-permute-start.3) | collective-permute-done | bytes 1310752 | tf_op jit(solution)/shard_map/ppermute | solution.py:195
  88.8 21.3 %collective-permute-done.4 = bf16[5,128,1024]{1,2,0:T(8,128)(2,1)S(1)} collective-permute-done((bf16[5,128,1024]{1,2,0:T(8,128)(2,1)S(1)}, bf16[5,128,1024]{1,2,0:T(8,128)(2,1)S(1)}, u32[]{:S(2)}, u32[]{:S(2)}) %collective-permute-start.4) | collective-permute-done | bytes 1310752 | tf_op jit(solution)/shard_map/ppermute | solution.py:195
  111.1 18.0 %collective-permute-done.5 = bf16[5,128,1024]{1,2,0:T(8,128)(2,1)} collective-permute-done((bf16[5,128,1024]{1,2,0:T(8,128)(2,1)S(1)}, bf16[5,128,1024]{1,2,0:T(8,128)(2,1)}, u32[]{:S(2)}, u32[]{:S(2)}) %collective-permute-start.5) | collective-permute-done | bytes 1310752 | tf_op jit(solution)/shard_map/ppermute | solution.py:195
  132.3 16.4 %collective-permute-done.6 = bf16[5,128,1024]{1,2,0:T(8,128)(2,1)} collective-permute-done((bf16[5,128,1024]{1,2,0:T(8,128)(2,1)}, bf16[5,128,1024]{1,2,0:T(8,128)(2,1)}, u32[]{:S(2)}, u32[]{:S(2)}) %collective-permute-start.6) | collective-permute-done | bytes 1310752 | tf_op jit(solution)/shard_map/ppermute | solution.py:195
  150.5 24.8 %collective-permute-done.7 = bf16[5,128,1024]{1,2,0:T(8,128)(2,1)} collective-permute-done((bf16[5,128,1024]{1,2,0:T(8,128)(2,1)}, bf16[5,128,1024]{1,2,0:T(8,128)(2,1)}, u32[]{:S(2)}, u32[]{:S(2)}) %collective-permute-start.7) | collective-permute-done | bytes 1310752 | tf_op jit(solution)/shard_map/ppermute | solution.py:195
  181.8 16.9 %collective-permute-done.8 = bf16[5,128,1024]{1,2,0:T(8,128)(2,1)} collective-permute-done((bf16[5,128,1024]{1,2,0:T(8,128)(2,1)}, bf16[5,128,1024]{1,2,0:T(8,128)(2,1)}, u32[]{:S(2)}, u32[]{:S(2)}) %collective-permute-start.8) | collective-permute-done | bytes 1310752 | tf_op jit(solution)/shard_map/ppermute | solution.py:195
  229.5 14.9 %fusion.24 = f32[4,1024,1024]{1,2,0:T(8,128)} fusion(bf16[5,2048,1024]{1,2,0:T(8,128)(2,1)} %constant_dynamic-update-slice_fusion, s32[]{:T(128)S(6)} %select_n.37, bf16[1024,1024]{1,0:T(8,128)(2,1)S(1)} %fusion.71), kind=kOutput, calls=%fused_computation.32 | convolution fusion | flops 8589934592 | bytes 29360132 | tf_op jit(solution)/shard_map/nd,kde->kne/dot_general | solution.py:203
  291.3 60.7 %while.22 = (s32[]{:T(128)}, f32[2,8,128,128]{3,2,1,0:T(8,128)S(1)}, f32[2,8,128,128]{3,2,1,0:T(8,128)}, f32[8]{0:T(128)S(1)}, pred[2]{0:T(512)(128)(4,1)S(1)}, /*index=5*/s32[]{:T(128)}, s32[]{:T(128)}) while((s32[]{:T(128)}, f32[2,8,128,128]{3,2,1,0:T(8,128)S(1)}, f32[2,8,128,128]{3,2,1,0:T(8,128)}, f32[8]{0:T(128)S(1)}, ...), condition=%wide.region_5.6_spmd.clone, body=%wide.region_4.5_spmd.clone.sunk | while | flops 1310739 | bytes 6291745 | solution.py:134
  293.6 12.8 %collective-permute-start = (bf16[2,8,128,128]{3,2,1,0:T(8,128)(2,1)}, bf16[2,8,128,128]{3,2,1,0:T(8,128)(2,1)}, u32[]{:S(2)}, u32[]{:S(2)}) collective-permute-start(bf16[2,8,128,128]{3,2,1,0:T(8,128)(2,1)} %fusion.146), channel_id=1, source_target_pairs={{0,8},{8,16},{16,24},{1,9},{9,17},{17,25},{2,10},{10,18},{18,26},{... | collective-permute-start | bytes 1572872 | tf_op jit(solution)/shard_map/while/body/eval_jaxpr/ppermute | solution.py:13
  361.2 17.0 %fusion.128 = f32[2,8,512,512]{3,2,1,0:T(8,128)} fusion(f32[2,512,8,128]{1,0,3,2:T(2,128)S(1)} %copy-done.15, f32[2,512,8,128]{1,0,3,2:T(2,128)S(1)} %copy-done.14), kind=kOutput, calls=%fused_computation.187 | convolution fusion | flops 6450839552 | bytes 25165824 | tf_op jit(solution)/shard_map/rthd,rshd->rhts/dot_general | solution.py:76
  378.3 23.8 %multiply_reduce_fusion.2 = (f32[2,512]{1,0:T(2,128)S(1)}, f32[2,512,8,128]{1,3,2,0:T(8,128)}) fusion(f32[2,512,8]{1,2,0:T(8,128)S(1)} %get-tuple-element.166, f32[2,8,128,512]{3,2,1,0:T(8,128)} %fusion.129, f32[2,512,8,128]{3,1,2,0:T(8,128)} %copy.119, f32[2,8,512,512]{3,2,1,0:T(8,128)} %fusion.128, f32[8,512,512]{2,1,0:T(8,128)} %multiply_exponential_fusion, ...), kind=kOutput, calls=%fused_computation.101 | convolution fusion | flops 6455032832 | bytes 38309888 | tf_op jit(solution)/shard_map/rhts,rshe->rthe/dot_general | solution.py:79
  429.1 21.3 %fusion.21 = f32[2,1024,2816]{2,1,0:T(8,128)} fusion(bf16[1,2,1024,2816]{3,2,1,0:T(8,128)(2,1)} %all-gather.5.cloned.1.call-done, f32[1024,1024]{1,0:T(8,128)} %get-tuple-element.159, f32[1024]{0:T(1024)S(1)} %get-tuple-element.149), kind=kOutput, calls=%fused_computation.31 | convolution fusion | flops 11813257216 | bytes 38801408 | tf_op jit(solution)/shard_map/nd,kdf->knf/dot_general | solution.py:224
  450.4 15.0 %fusion.47 = (bf16[1,1024,2816]{2,1,0:T(8,128)(2,1)}, bf16[1,1024,2816]{2,1,0:T(8,128)(2,1)}) fusion(f32[2,1024,2816]{2,1,0:T(8,128)} %fusion.21, bf16[1024,1024]{1,0:T(8,128)(2,1)S(1)} %bitcast.231, bf16[1,2816,1024]{2,1,0:T(8,128)(2,1)} %all-gather.7.cloned.1.call-done), kind=kOutput, calls=%fused_computation.54 | convolution fusion | flops 5922881536 | bytes 42467328 | tf_op jit(solution)/shard_map/nd,fd->nf/dot_general | solution.py:290
  465.5 20.3 %fusion.68 = (f32[1024]{0:T(1024)S(1)}, f32[1024,1024,1]{1,0,2:T(8,128)}) fusion(f32[1024,1024]{1,0:T(8,128)} %get-tuple-element.159, bf16[1,2,1024,2816]{3,2,1,0:T(8,128)(2,1)} %all-gather.5.cloned.1.call-done, bf16[1,1024,2816]{2,1,0:T(8,128)(2,1)} %get-tuple-element.140, bf16[1,1024,2816]{2,1,0:T(8,128)(2,1)} %get-tuple-element.139), kind=kOutput, calls=%fused_computation.81 | convolution fusion | flops 11819023360 | bytes 31461376 | tf_op jit(solution)/shard_map/knf,kdf->nd/dot_general | solution.py:298
  510.4 19.9 %fusion.8 = f32[2,8,128,512]{3,2,1,0:T(8,128)} fusion(f32[2,8,512,512]{3,2,1,0:T(8,128)} %fusion.128, f32[8,512,512]{2,1,0:T(8,128)} %multiply_exponential_fusion, pred[2,512,512]{2,1,0:T(8,128)(4,1)S(1)} %copy-done.17, f32[2,512,8,128]{1,0,3,2:T(2,128)} %reshape.344), kind=kOutput, calls=%fused_computation.12 | convolution fusion | flops 6450839552 | bytes 34078720 | tf_op jit(solution)/shard_map/rhts,rthe->rshe/dot_general | solution.py:119
  539.2 16.0 %fusion.80 = f32[2,8,512,512]{3,2,1,0:T(8,128)} fusion(f32[2,512,8,128]{3,1,2,0:T(8,128)S(1)} %copy-done.5, f32[2,512,8,128]{1,0,3,2:T(2,128)S(1)} %copy-done.6), kind=kOutput, calls=%fused_computation.109 | convolution fusion | flops 6442450944 | bytes 25165824 | tf_op jit(solution)/shard_map/rthe,rshe->rhts/dot_general | solution.py:105
  561.1 42.1 %while.23 = (s32[]{:T(128)}, f32[2,8,128,128]{3,2,1,0:T(8,128)S(1)}, f32[2,8,128,128]{3,2,1,0:T(8,128)S(1)}, f32[8]{0:T(128)S(1)}, pred[2]{0:T(512)(128)(4,1)S(1)}, /*index=5*/s32[]{:T(128)}, s32[]{:T(128)}) while((s32[]{:T(128)}, f32[2,8,128,128]{3,2,1,0:T(8,128)S(1)}, f32[2,8,128,128]{3,2,1,0:T(8,128)S(1)}, f32[8]{0:T(128)S(1)}, ...), condition=%wide.region_11.12_spmd.clone, body=%wide.region_10.11_spmd.clone.sunk | while | flops 1310739 | bytes 6291745 | solution.py:143
  563.5 12.9 %collective-permute-done.1 = bf16[2,8,128,128]{3,2,1,0:T(8,128)(2,1)S(1)} collective-permute-done((bf16[2,8,128,128]{3,2,1,0:T(8,128)(2,1)}, bf16[2,8,128,128]{3,2,1,0:T(8,128)(2,1)S(1)}, u32[]{:S(2)}, u32[]{:S(2)}) %collective-permute-start.1) | collective-permute-done | bytes 524320 | tf_op jit(solution)/shard_map/while/body/eval_jaxpr/ppermute | solution.py:13
  578.8 11.5 %collective-permute-done.1 = bf16[2,8,128,128]{3,2,1,0:T(8,128)(2,1)S(1)} collective-permute-done((bf16[2,8,128,128]{3,2,1,0:T(8,128)(2,1)}, bf16[2,8,128,128]{3,2,1,0:T(8,128)(2,1)S(1)}, u32[]{:S(2)}, u32[]{:S(2)}) %collective-permute-start.1) | collective-permute-done | bytes 524320 | tf_op jit(solution)/shard_map/while/body/eval_jaxpr/ppermute | solution.py:13
  621.1 27.9 %fusion.11 = f32[2,8,128,512]{3,2,1,0:T(8,128)} fusion(f32[2,8,512,512]{3,2,1,0:T(8,128)} %fusion.80, f32[8,512,512]{2,1,0:T(8,128)} %multiply_exponential_fusion, pred[2,512,512]{2,1,0:T(8,128)(4,1)S(1)} %copy-done.17, f32[2,512,8,128]{1,0,3,2:T(2,128)} %squeeze.13), kind=kOutput, calls=%fused_computation.15 | convolution fusion | flops 6455033856 | bytes 34078720 | tf_op jit(solution)/shard_map/rhts,rshd->rthd/dot_general | solution.py:107
  669.4 21.8 %fusion.63 = f32[2,512,8,128]{1,3,2,0:T(8,128)} fusion(f32[2,8,128,512]{3,2,1,0:T(8,128)} %fusion.133, f32[2,8,512,512]{3,2,1,0:T(8,128)} %fusion.80, f32[8,512,512]{2,1,0:T(8,128)} %multiply_exponential_fusion, pred[2,512,512]{2,1,0:T(8,128)(4,1)S(1)} %copy-done.17, f32[2,512,8]{1,2,0:T(8,128)S(1)} %copy-done.37, f32[2,512,8,128]{1,0,3,2:T(2,128)} %squeeze.12), kind=kOutput, calls=%fused_computation.72 | convolution fusion | flops 6457131008 | bytes 38305792 | tf_op jit(solution)/shard_map/rhts,rthd->rshd/dot_general | solution.py:113
  726.3 14.9 %copy.151 = bf16[4,1024,1024]{2,0,1:T(4,128)(2,1)} copy(bf16[4,1024,1024]{1,2,0:T(8,128)(2,1)} %convert_bitcast_fusion.1) | data formatting | bytes 16777216
  741.2 12.1 %copy.160 = bf16[128,8,4,1024]{3,1,2,0:T(8,128)(2,1)} copy(bf16[128,8,4,1024]{3,2,1,0:T(4,128)(2,1)} %bitcast.225) | data formatting | bytes 16777216
  753.4 19.5 %convert_bitcast_fusion = bf16[2,1024,2816]{1,2,0:T(8,128)(2,1)} fusion(bf16[1,1024,2816]{2,1,0:T(8,128)(2,1)} %get-tuple-element.140, bf16[1,1024,2816]{2,1,0:T(8,128)(2,1)} %get-tuple-element.139, f32[1024,1024]{1,0:T(8,128)} %get-tuple-element.159, f32[1024]{0:T(1024)S(1)} %get-tuple-element.149), kind=kOutput, calls=%fused_computation.28 | convolution fusion | flops 11824791552 | bytes 27267072 | tf_op jit(solution)/shard_map/nd,knf->kdf/dot_general | solution.py:295
  772.9 29.3 %copy.155 = bf16[2,1024,2816]{2,0,1:T(2,128)(2,1)} copy(bf16[2,1024,2816]{1,2,0:T(8,128)(2,1)} %convert_bitcast_fusion) | data formatting | bytes 23068672
  815.1 16.0 %fusion.51 = bf16[2816,1024]{1,0:T(8,128)(2,1)} fusion(bf16[1024,1024]{1,0:T(8,128)(2,1)S(1)} %bitcast.232, f32[2,1024,2816]{2,1,0:T(8,128)} %fusion.21), kind=kOutput, calls=%fused_computation.58 | convolution fusion | flops 5914230784 | bytes 30932992 | tf_op jit(solution)/shard_map/nf,nd->fd/dot_general | solution.py:288
  837.4 77.1 %reduce-scatter.17.cloned.1.call-done = bf16[128,5632]{1,0:T(8,128)(2,1)} async-done(((bf16[1024,5632]{1,0:T(8,128)(2,1)}), bf16[128,5632]{1,0:T(8,128)(2,1)}) %reduce-scatter.17.cloned.1.call-update) | async-done | bytes 1441808
  921.1 55.9 %reduce-scatter.11.cloned.1.call-done = bf16[352,1024]{1,0:T(8,128)(2,1)} async-done(((bf16[2816,1024]{1,0:T(8,128)(2,1)}), bf16[352,1024]{1,0:T(8,128)(2,1)}) %reduce-scatter.11.cloned.1.call-update) | async-done | bytes 720912 | tf_op jit(solution)/shard_map/reduce_scatter | solution.py:157
  977.0 14.4 %fusion.60 = (f32[1024]{0:T(1024)S(1)}, f32[1024,1024,1]{1,0,2:T(8,128)S(1)}) fusion(bf16[2,512,1024]{2,1,0:T(8,128)(2,1)S(1)} %copy-done.11, bf16[5,2048,1024]{1,2,0:T(8,128)(2,1)} %constant_dynamic-update-slice_fusion, s32[]{:T(128)S(6)} %select_n.37, bf16[1,1024,1024]{1,2,0:T(8,128)(2,1)} %get-tuple-element.147, ...), kind=kOutput, calls=%fused_computation.67 | convolution fusion | flops 8605662208 | bytes 23072772 | tf_op jit(solution)/shard_map/kne,kde->nd/dot_general | solution.py:338
  994.9 13.5 %add_convert_fusion = bf16[1024,1024]{1,0:T(8,128)(2,1)} fusion(f32[1024,1024]{1,0:T(8,128)S(1)} %copy-done.13, bf16[1,2816,1024]{2,1,0:T(8,128)(2,1)} %all-gather.7.cloned.1.call-done, f32[2,1024,2816]{2,1,0:T(8,128)} %fusion.21), kind=kOutput, calls=%fused_computation.97 | convolution fusion | flops 5913444352 | bytes 35127296 | tf_op jit(solution)/shard_map/dot_general | solution.py:17
  1008.3 104.7 %all-reduce.3.cloned.1.call-done = (bf16[1,2,128,2816]{2,3,1,0:T(8,128)(2,1)}, bf16[1,128,1024]{1,2,0:T(8,128)(2,1)}, bf16[4,128,1024]{1,2,0:T(8,128)(2,1)}, bf16[1,352,1024]{2,1,0:T(8,128)(2,1)}) async-done(((bf16[1,2,128,2816]{2,3,1,0:T(8,128)(2,1)}, bf16[1,128,1024]{1,2,0:T(8,128)(2,1)}, bf16[4,128,1024]{1,2,0:T(8,128)(2,1)}, bf16[1,352,1024]{2,1,0:T(8,128)(2,1)}), (bf16[1,2,128,2816]{2,3,1,0:T(8,128)(2,1)}, ...) | async-done | bytes 3473424 | tf_op jit(solution)/shard_map/psum | solution.py:164
  (230 shorter events, 354.7 us)
Async XLA Ops:
  7.2 421.9 %all-gather.5.cloned.1.call-start = ((), (), s32[]{:S(2)}) async-start(), calls=%async_computation.5 | async-start | bytes 12976128 | tf_op jit(solution)/shard_map/all_gather | solution.py:199
  10.3 121.3 %copy-start.44 = (s32[2,4]{1,0:T(2,128)S(1)}, s32[2,4]{1,0:T(2,128)}, u32[]{:S(2)}) copy-start(s32[2,4]{1,0:T(2,128)} %param.16) | copy-start | bytes 100
  10.3 139.6 %copy-start.45 = (f32[1,8]{1,0:T(1,128)S(1)}, f32[1,8]{1,0:T(1,128)}, u32[]{:S(2)}) copy-start(f32[1,8]{1,0:T(1,128)} %param.15) | copy-start | bytes 100
  10.3 139.6 %copy-start.10 = (bf16[2,512,1024]{2,1,0:T(8,128)(2,1)S(1)}, bf16[2,512,1024]{2,1,0:T(8,128)(2,1)}, u32[]{:S(2)}) copy-start(bf16[2,512,1024]{2,1,0:T(8,128)(2,1)} %param.11) | copy-start | bytes 6291460
  10.3 440.1 %all-gather.7.cloned.1.call-start = ((), (), s32[]{:S(2)}) async-start(), calls=%async_computation.6 | async-start | bytes 6488064 | tf_op jit(solution)/shard_map/all_gather | solution.py:200
  13.3 32.8 %collective-permute-start.2 = (bf16[5,128,1024]{1,2,0:T(8,128)(2,1)}, bf16[5,128,1024]{1,2,0:T(8,128)(2,1)S(1)}, u32[]{:S(2)}, u32[]{:S(2)}) collective-permute-start(bf16[5,128,1024]{1,2,0:T(8,128)(2,1)} %bitcast.226), channel_id=1, source_target_pairs={{0,1},{1,2},{2,3},{3,4},{4,5},{5,6},{6,7},{7,0},{8,9},{9,10},{10,1... | collective-permute-start | bytes 3932168 | tf_op jit(solution)/shard_map/ppermute | solution.py:195
  47.2 36.1 %collective-permute-start.3 = (bf16[5,128,1024]{1,2,0:T(8,128)(2,1)S(1)}, bf16[5,128,1024]{1,2,0:T(8,128)(2,1)S(1)}, u32[]{:S(2)}, u32[]{:S(2)}) collective-permute-start(bf16[5,128,1024]{1,2,0:T(8,128)(2,1)S(1)} %collective-permute-done.2), channel_id=1, source_target_pairs={{0,1},{1,2},{2,3},{3,4},{4,5},{5,6},{6,7},{7,0},{8,9},{9,10},{10,1... | collective-permute-start | bytes 3932168 | tf_op jit(solution)/shard_map/ppermute | solution.py:195
  84.3 25.7 %collective-permute-start.4 = (bf16[5,128,1024]{1,2,0:T(8,128)(2,1)S(1)}, bf16[5,128,1024]{1,2,0:T(8,128)(2,1)S(1)}, u32[]{:S(2)}, u32[]{:S(2)}) collective-permute-start(bf16[5,128,1024]{1,2,0:T(8,128)(2,1)S(1)} %collective-permute-done.3), channel_id=1, source_target_pairs={{0,1},{1,2},{2,3},{3,4},{4,5},{5,6},{6,7},{7,0},{8,9},{9,10},{10,1... | collective-permute-start | bytes 3932168 | tf_op jit(solution)/shard_map/ppermute | solution.py:195
  111.1 18.0 %collective-permute-start.5 = (bf16[5,128,1024]{1,2,0:T(8,128)(2,1)S(1)}, bf16[5,128,1024]{1,2,0:T(8,128)(2,1)}, u32[]{:S(2)}, u32[]{:S(2)}) collective-permute-start(bf16[5,128,1024]{1,2,0:T(8,128)(2,1)S(1)} %collective-permute-done.4), channel_id=1, source_target_pairs={{0,1},{1,2},{2,3},{3,4},{4,5},{5,6},{6,7},{7,0},{8,9},{9,10},{10,1... | collective-permute-start | bytes 3932168 | tf_op jit(solution)/shard_map/ppermute | solution.py:195
  129.2 19.5 %collective-permute-start.6 = (bf16[5,128,1024]{1,2,0:T(8,128)(2,1)}, bf16[5,128,1024]{1,2,0:T(8,128)(2,1)}, u32[]{:S(2)}, u32[]{:S(2)}) collective-permute-start(bf16[5,128,1024]{1,2,0:T(8,128)(2,1)} %collective-permute-done.5), channel_id=1, source_target_pairs={{0,1},{1,2},{2,3},{3,4},{4,5},{5,6},{6,7},{7,0},{8,9},{9,10},{10,1... | collective-permute-start | bytes 3932168 | tf_op jit(solution)/shard_map/ppermute | solution.py:195
  131.5 700.3 %reduce-scatter.15.cloned.1.call-start = ((), (), s32[]{:S(2)}) async-start(), calls=%async_computation.8 | async-start | bytes 2359296
  148.6 26.7 %collective-permute-start.7 = (bf16[5,128,1024]{1,2,0:T(8,128)(2,1)}, bf16[5,128,1024]{1,2,0:T(8,128)(2,1)}, u32[]{:S(2)}, u32[]{:S(2)}) collective-permute-start(bf16[5,128,1024]{1,2,0:T(8,128)(2,1)} %collective-permute-done.6), channel_id=1, source_target_pairs={{0,1},{1,2},{2,3},{3,4},{4,5},{5,6},{6,7},{7,0},{8,9},{9,10},{10,1... | collective-permute-start | bytes 3932168 | tf_op jit(solution)/shard_map/ppermute | solution.py:195
  175.3 23.4 %collective-permute-start.8 = (bf16[5,128,1024]{1,2,0:T(8,128)(2,1)}, bf16[5,128,1024]{1,2,0:T(8,128)(2,1)}, u32[]{:S(2)}, u32[]{:S(2)}) collective-permute-start(bf16[5,128,1024]{1,2,0:T(8,128)(2,1)} %collective-permute-done.7), channel_id=1, source_target_pairs={{0,1},{1,2},{2,3},{3,4},{4,5},{5,6},{6,7},{7,0},{8,9},{9,10},{10,1... | collective-permute-start | bytes 3932168 | tf_op jit(solution)/shard_map/ppermute | solution.py:195
  175.6 106.2 %copy-start.36 = (f32[2,512,8]{1,2,0:T(8,128)}, f32[2,512,8]{1,2,0:T(8,128)S(1)}, u32[]{:S(2)}) copy-start(f32[2,512,8]{1,2,0:T(8,128)S(1)} %get-tuple-element.167) | copy-start | bytes 98308
  177.3 52.2 %copy-start.30 = (bf16[1024,1024]{1,0:T(8,128)(2,1)}, bf16[1024,1024]{1,0:T(8,128)(2,1)S(1)}, u32[]{:S(2)}) copy-start(bf16[1024,1024]{1,0:T(8,128)(2,1)S(1)} %fusion.71) | copy-start | bytes 6291460
  293.6 22.6 %collective-permute-start = (bf16[2,8,128,128]{3,2,1,0:T(8,128)(2,1)}, bf16[2,8,128,128]{3,2,1,0:T(8,128)(2,1)}, u32[]{:S(2)}, u32[]{:S(2)}) collective-permute-start(bf16[2,8,128,128]{3,2,1,0:T(8,128)(2,1)} %fusion.146), channel_id=1, source_target_pairs={{0,8},{8,16},{16,24},{1,9},{9,17},{17,25},{2,10},{10,18},{18,26},{... | collective-permute-start | bytes 1572872 | tf_op jit(solution)/shard_map/while/body/eval_jaxpr/ppermute | solution.py:13
  319.7 16.2 %collective-permute-start = (bf16[2,8,128,128]{3,2,1,0:T(8,128)(2,1)}, bf16[2,8,128,128]{3,2,1,0:T(8,128)(2,1)}, u32[]{:S(2)}, u32[]{:S(2)}) collective-permute-start(bf16[2,8,128,128]{3,2,1,0:T(8,128)(2,1)} %fusion.146), channel_id=1, source_target_pairs={{0,8},{8,16},{16,24},{1,9},{9,17},{17,25},{2,10},{10,18},{18,26},{... | collective-permute-start | bytes 1572872 | tf_op jit(solution)/shard_map/while/body/eval_jaxpr/ppermute | solution.py:13
  339.3 11.6 %collective-permute-start = (bf16[2,8,128,128]{3,2,1,0:T(8,128)(2,1)}, bf16[2,8,128,128]{3,2,1,0:T(8,128)(2,1)}, u32[]{:S(2)}, u32[]{:S(2)}) collective-permute-start(bf16[2,8,128,128]{3,2,1,0:T(8,128)(2,1)} %fusion.146), channel_id=1, source_target_pairs={{0,8},{8,16},{16,24},{1,9},{9,17},{17,25},{2,10},{10,18},{18,26},{... | collective-permute-start | bytes 1572872 | tf_op jit(solution)/shard_map/while/body/eval_jaxpr/ppermute | solution.py:13
  429.1 21.3 %copy-start.33 = (bf16[2,512,1024]{2,1,0:T(8,128)(2,1)S(1)}, bf16[2,512,1024]{2,1,0:T(8,128)(2,1)}, u32[]{:S(2)}) copy-start(bf16[2,512,1024]{2,1,0:T(8,128)(2,1)} %param.17) | copy-start | bytes 6291460
  539.2 16.0 %copy-start.1 = (f32[128,8,2,512]{3,1,2,0:T(8,128)S(1)}, f32[128,8,2,512]{3,1,2,0:T(8,128)}, u32[]{:S(2)}) copy-start(f32[128,8,2,512]{3,1,2,0:T(8,128)} %copy.159) | copy-start | bytes 12582916
  539.2 16.0 %copy-start.3 = (f32[1024,1024]{1,0:T(8,128)S(1)}, f32[1024,1024]{1,0:T(8,128)}, u32[]{:S(2)}) copy-start(f32[1024,1024]{1,0:T(8,128)} %copy-done.2) | copy-start | bytes 12582916
  562.2 14.1 %collective-permute-start.1 = (bf16[2,8,128,128]{3,2,1,0:T(8,128)(2,1)}, bf16[2,8,128,128]{3,2,1,0:T(8,128)(2,1)S(1)}, u32[]{:S(2)}, u32[]{:S(2)}) collective-permute-start(bf16[2,8,128,128]{3,2,1,0:T(8,128)(2,1)} %fusion.147), channel_id=1, source_target_pairs={{8,0},{16,8},{24,16},{9,1},{17,9},{25,17},{10,2},{18,10},{26,18},{... | collective-permute-start | bytes 1572872 | tf_op jit(solution)/shard_map/while/body/eval_jaxpr/ppermute | solution.py:13
  577.5 12.8 %collective-permute-start.1 = (bf16[2,8,128,128]{3,2,1,0:T(8,128)(2,1)}, bf16[2,8,128,128]{3,2,1,0:T(8,128)(2,1)S(1)}, u32[]{:S(2)}, u32[]{:S(2)}) collective-permute-start(bf16[2,8,128,128]{3,2,1,0:T(8,128)(2,1)} %fusion.147), channel_id=1, source_target_pairs={{8,0},{16,8},{24,16},{9,1},{17,9},{25,17},{10,2},{18,10},{26,18},{... | collective-permute-start | bytes 1572872 | tf_op jit(solution)/shard_map/while/body/eval_jaxpr/ppermute | solution.py:13
  591.5 11.3 collective-permute-start.1
  621.1 27.9 %copy-start.9 = (f32[2,8,128,128]{3,2,1,0:T(8,128)S(1)}, f32[2,8,128,128]{3,2,1,0:T(8,128)}, u32[]{:S(2)}) copy-start(f32[2,8,128,128]{3,2,1,0:T(8,128)} %copy-done.8) | copy-start | bytes 3145732
  705.3 9.9 copy-start.27
  705.3 128.4 %reduce-scatter.13.cloned.1.call-start = ((), (), s32[]{:S(2)}) async-start(), calls=%async_computation.7 | async-start | bytes 9437184
  753.3 161.2 %reduce-scatter.17.cloned.1.call-start = ((), (), s32[]{:S(2)}) async-start(), calls=%async_computation.9 | async-start | bytes 12976128
  813.6 163.4 %reduce-scatter.11.cloned.1.call-start = ((), (), s32[]{:S(2)}) async-start(), calls=%async_computation.4 | async-start | bytes 6488064 | tf_op jit(solution)/shard_map/reduce_scatter | solution.py:157
  831.2 281.9 %all-reduce.3.cloned.1.call-start = ((), (), s32[]{:S(2)}) async-start(), calls=%async_computation.10 | async-start | bytes 6946816 | tf_op jit(solution)/shard_map/psum | solution.py:164
  837.4 139.5 %copy-start.11 = (bf16[2,512,1024]{2,1,0:T(8,128)(2,1)S(1)}, bf16[2,512,1024]{2,1,0:T(8,128)(2,1)}, u32[]{:S(2)}) copy-start(bf16[2,512,1024]{2,1,0:T(8,128)(2,1)} %param.11) | copy-start | bytes 6291460
  977.0 14.4 %copy-start.4 = (f32[1024,1024]{1,0:T(8,128)S(1)}, f32[1024,1024]{1,0:T(8,128)}, u32[]{:S(2)}) copy-start(f32[1024,1024]{1,0:T(8,128)} %copy-done.2) | copy-start | bytes 12582916
  (34 other events, 198.3 us)
Sparse Core Ops, SparseCore 0:
  10.5 91.6 all-gather.4
  131.7 58.1 all-gather.6
  705.4 40.7 reduce-scatter.14
  753.4 70.9 reduce-scatter.12
  827.7 86.7 reduce-scatter.16
  917.9 59.0 reduce-scatter.10
  980.3 132.6 all-reduce.2
